TPU v7x, 32 devices: a whole 2x2x4 slice. The times are simulated.
32 devices in a mesh: row: 16 (over z, y, x), col: 2 (over core).
Axes of the slice: x: 2, y: 2, z: 4, core: 2. Of those that a mesh axis runs over, the one named last changes fastest.
Arguments:
- acts: bfloat16 [2048, 8192], P('row'), may hold values from -22 to 22
- out_grads: bfloat16 [2048, 4096], P('row', 'col'), may hold values from -0.198873782 to 0.198873782
- weight: float32 [8192, 4096], P('row', 'col'), may hold values from -30 to 30
- row_state: float32 [8192], P('row'), may hold values from 0.002 to 2
- col_state: float32 [4096], P('col'), may hold values from 0.01 to 0.3
Outputs:
- new_weight: float32 [8192, 4096], P('row', 'col')
- update: float32 [8192, 4096], P('row', 'col')
- row_moment: float32 [8192], P('row')
- col_moment: float32 [4096], P('col')
All inputs are finite; a program needn't handle non-finite values.
Results may differ from a plain program's by a relative error of at most 0.0003.
Values may be sent and summed in bfloat16 or wider, within the bound.
No kernel may reach another device: no remote copies, remote signals or barrier semaphores. Data moves between devices by JAX's collectives and lax.ppermute only.
A program may use at most 64 MiB of HBM per device.

v0:
```python
import jax
import jax.numpy as jnp
from jax import lax
from jax.sharding import PartitionSpec as P

decay_rate = 0.85
floor_eps = 1e-30
relative_rate = 0.05


def per_device(acts, out_grads, weight, row_state, col_state):
    n_col = lax.axis_size("col")
    width = acts.shape[1]
    cols_here = out_grads.shape[1]
    cols_all = cols_here * n_col
    columns = lax.all_to_all(acts, "row", split_axis=1, concat_axis=0, tiled=True)
    gradient = lax.dot_general(
        columns,
        lax.all_gather(out_grads, "row", axis=0, tiled=True),
        (((0,), (0,)), ((), ())),
        preferred_element_type=jnp.float32,
    )
    squares = gradient * gradient + floor_eps
    row_squares = jnp.sum(squares, axis=1)
    col_squares = jnp.sum(squares, axis=0)
    weight_part = jnp.sum(weight * weight)
    row_total = lax.psum(row_squares, "col")
    col_total = lax.psum(col_squares, "row")
    weight_total = lax.psum(weight_part, ("row", "col"))
    row_moment = decay_rate * row_state + (1.0 - decay_rate) * (row_total / cols_all)
    col_moment = decay_rate * col_state + (1.0 - decay_rate) * (col_total / width)
    unclipped = gradient * lax.rsqrt(row_moment[:, None] * col_moment[None, :])
    update_total = lax.psum(jnp.sum(unclipped * unclipped), ("row", "col"))
    count_all = width * cols_all
    clip_factor = jnp.maximum(1.0, jnp.sqrt(update_total / count_all))
    update = unclipped / clip_factor
    step_size = relative_rate * jnp.sqrt(weight_total / count_all + 1e-06)
    new_weight = weight - step_size * update
    return (new_weight, update, row_moment, col_moment)


def solution(mesh):
    return jax.shard_map(
        per_device,
        mesh=mesh,
        in_specs=(P("row", None), P("row", "col"), P("row", "col"), P("row"), P("col")),
        out_specs=(P("row", "col"), P("row", "col"), P("row"), P("col")),
        check_vma=False,
    )
```

profile of v0, /device:TPU:12, one launch (start us, length us, event | category | flops | bytes accessed | tf_op | source)
XLA Modules:
  0.0 269.7 jit_solution(2994545322753481755)
XLA Ops:
  7.2 0.0 all-gather.2.cloned.1.call-start
  7.2 0.7 all-gather.2.cloned.1.call-update
  7.9 4.1 %copy.9 = bf16[128,8192]{0,1:T(8,128)(2,1)} copy(bf16[128,8192]{1,0:T(8,128)(2,1)} %param.5) | data formatting | bytes 4194304 | tf_op args[0]
  12.0 7.2 %all-to-all-start = ((bf16[128,16,512]{0,2,1:T(8,128)(2,1)}), bf16[128,16,512]{0,2,1:T(8,128)(2,1)S(1)}, u32[]{:S(2)}, u32[]{:S(2)}) async-start(bf16[128,16,512]{0,2,1:T(8,128)(2,1)} %bitcast.6), calls=%async_computation | async-start | bytes 4194304 | tf_op jit(solution)/shard_map/all_to_all | solution.py:16
  19.1 4.1 %multiply_reduce_fusion.1 = f32[]{:T(128)} fusion(f32[512,2048]{1,0:T(8,128)} %param.7), kind=kLoop, calls=%fused_computation.4 | loop fusion | flops 2097151 | bytes 4194308 | tf_op jit(solution)/shard_map/reduce_sum | solution.py:26
  23.3 77.5 %all-to-all-done = bf16[128,16,512]{0,2,1:T(8,128)(2,1)S(1)} async-done(((bf16[128,16,512]{0,2,1:T(8,128)(2,1)}), bf16[128,16,512]{0,2,1:T(8,128)(2,1)S(1)}, u32[]{:S(2)}, u32[]{:S(2)}) %all-to-all-start) | async-done | bytes 2097184 | tf_op jit(solution)/shard_map/all_to_all | solution.py:16
  100.7 2.6 copy.10
  103.3 52.0 %all-gather.2.cloned.1.call-done = bf16[2048,2048]{1,0:T(8,128)(2,1)} async-done(((bf16[128,2048]{1,0:T(8,128)(2,1)}), bf16[2048,2048]{1,0:T(8,128)(2,1)}) %all-gather.2.cloned.1.call-update) | async-done | bytes 8388624 | tf_op jit(solution)/shard_map/all_gather | solution.py:19
  155.4 0.0 copy-start.2
  155.4 0.0 copy-start.3
  155.4 10.9 %fusion.1 = (f32[512]{0:T(512)S(1)}, f32[2048]{0:T(1024)S(1)}, f32[512,2048]{1,0:T(8,128)}) fusion(bf16[2048,512]{1,0:T(8,128)(2,1)} %bitcast.7, bf16[2048,2048]{1,0:T(8,128)(2,1)} %all-gather.2.cloned.1.call-done), kind=kOutput, calls=%fused_computation.6 | convolution fusion | flops 4299159040 | bytes 14690304 | tf_op jit(solution)/shard_map/dot_general | solution.py:17
  166.3 30.4 %psum.30 = f32[2048]{0:T(1024)S(1)} all-reduce(f32[2048]{0:T(1024)S(1)} %get-tuple-element.5), channel_id=1, replica_groups=mesh['row'=16,'col'=2] {'row'}, use_global_device_ids=true, to_apply=%region_5.0 | all-reduce | flops 2048 | bytes 16384 | tf_op jit(solution)/shard_map/psum | solution.py:28
  196.7 2.5 psum.29
  199.2 0.0 copy-done.2
  199.2 0.0 copy-done.3
  199.2 0.0 copy-start
  199.2 0.0 copy-start.1
  199.2 4.1 %multiply_reduce_fusion = f32[]{:T(128)} fusion(f32[512,2048]{1,0:T(8,128)} %get-tuple-element.10, f32[2048]{0:T(1024)S(1)} %multiply_add_fusion.1, f32[512]{0:T(512)S(1)} %multiply_add_fusion.2), kind=kLoop, calls=%fused_computation.1 | loop fusion | flops 4194303 | bytes 4204548 | tf_op jit(solution)/shard_map/reduce_sum | solution.py:33
  203.3 49.3 %all-reduce = (f32[]{:T(128)}, f32[]{:T(128)}) all-reduce(f32[]{:T(128)} %multiply_reduce_fusion, f32[]{:T(128)} %multiply_reduce_fusion.1), channel_id=1, replica_groups=mesh['row'=16,'col'=2] {'row','col'}, use_global_device_ids=true, to_apply=%region_7.0 | all-reduce | flops 2 | bytes 16 | tf_op jit(solution)/shard_map/psum | solution.py:33
  253.9 8.9 %multiply_subtract_fusion = (f32[512,2048]{1,0:T(8,128)}, f32[512,2048]{1,0:T(8,128)}) fusion(f32[512,2048]{1,0:T(8,128)} %param.7, f32[]{:T(128)S(6)} %mul_shard_map.3, f32[]{:T(128)S(6)} %max_shard_map.3, f32[512,2048]{1,0:T(8,128)} %get-tuple-element.10, f32[2048]{0:T(1024)S(1)} %multiply_add_fusion.1, f32[512]{0:T(512)S(1)} %multiply_add_fusion.2), kind=kLoop, calls=%fused_computation | loop fusion | flops 5242880 | bytes 16787464 | tf_op jit(solution)/shard_map/sub | solution.py:38
  262.9 0.0 copy-done
  262.9 0.0 copy-done.1
  (2 shorter events, 0.0 us)
Async XLA Ops:
  7.2 148.2 %all-gather.2.cloned.1.call-start = ((), (), s32[]{:S(2)}) async-start(), calls=%async_computation.1 | async-start | bytes 8912896 | tf_op jit(solution)/shard_map/all_gather | solution.py:19
  12.0 88.8 %all-to-all-start = ((bf16[128,16,512]{0,2,1:T(8,128)(2,1)}), bf16[128,16,512]{0,2,1:T(8,128)(2,1)S(1)}, u32[]{:S(2)}, u32[]{:S(2)}) async-start(bf16[128,16,512]{0,2,1:T(8,128)(2,1)} %bitcast.6), calls=%async_computation | async-start | bytes 4194304 | tf_op jit(solution)/shard_map/all_to_all | solution.py:16
  155.4 43.8 %copy-start.2 = (f32[2048]{0:T(1024)S(1)}, f32[2048]{0:T(1024)}, u32[]{:S(2)}) copy-start(f32[2048]{0:T(1024)} %param.9) | copy-start | bytes 24580
  155.4 43.8 %copy-start.3 = (f32[512]{0:T(512)S(1)}, f32[512]{0:T(512)}, u32[]{:S(2)}) copy-start(f32[512]{0:T(512)} %param.8) | copy-start | bytes 6148
  199.2 63.7 %copy-start = (f32[2048]{0:T(1024)}, f32[2048]{0:T(1024)S(1)}, u32[]{:S(2)}) copy-start(f32[2048]{0:T(1024)S(1)} %multiply_add_fusion.1) | copy-start | bytes 24580
  199.2 63.6 %copy-start.1 = (f32[512]{0:T(512)}, f32[512]{0:T(512)S(1)}, u32[]{:S(2)}) copy-start(f32[512]{0:T(512)S(1)} %multiply_add_fusion.2) | copy-start | bytes 6148
Sparse Core Ops, SparseCore 0:
  10.7 144.5 all-gather.1
where the time goes:
time: 270 us
  waiting for transfers between devices  130 us (48%)
  blocking collectives  82.2 us (30%)
  other arithmetic  17.1 us (6%)
  between operations  15.4 us (6%)
  matrix products  10.9 us (4%)
  starting transfers between devices  7.21 us (3%)
  local copies, waits for them, and re-layouts  6.67 us (2%)
    all_to_all x1, waiting for transfers between devices, per_device(): lax.all_to_all(acts, 'row', split_axis=1, concat_axis=0, tiled=True)  77.5 us
    all_gather x1, waiting for transfers between devices, per_device(): lax.all_gather(out_grads, 'row', axis=0, tiled=True)  52 us
    psum x1, blocking collectives, per_device(): update_total = lax.psum(jnp.sum(unclipped * unclipped), ('row', 'col'))  49.3 us
    psum x1, blocking collectives, per_device(): col_total = lax.psum(col_squares, 'row')  30.4 us
    dot_general x1, matrix products, per_device(): lax.dot_general(columns, lax.all_gather(out_grads, 'row', axis=0, tiled=T...  10.9 us
    sub x1, other arithmetic, per_device(): new_weight = weight - step_size * update  8.93 us
    all_to_all x1, starting transfers between devices, per_device(): lax.all_to_all(acts, 'row', split_axis=1, concat_axis=0, tiled=True)  7.17 us
  transfers between devices with their start and end apart: 2, of which 2 were waited for; matrix products, arithmetic and copies ran while one was open for 4% of the time, Pallas kernels for 0%

commit v1 on v0

--- a/solution.py
+++ b/solution.py
@@ -13,7 +13,10 @@
     width = acts.shape[1]
     cols_here = out_grads.shape[1]
     cols_all = cols_here * n_col
-    columns = lax.all_to_all(acts, "row", split_axis=1, concat_axis=0, tiled=True)
+    columns = jnp.concatenate(
+        lax.all_to_all(jnp.stack(jnp.split(acts, lax.axis_size("row"), axis=1)), "row", 0, 0),
+        axis=0,
+    )
     gradient = lax.dot_general(
         columns,
         lax.all_gather(out_grads, "row", axis=0, tiled=True),

time: 270 us -> 268 us (level)
  waiting for transfers between devices: 130 us -> 119 us
  local copies, waits for them, and re-layouts: 6.67 us -> 17 us
    unnamed x9 -> x25, local copies, waits for them, and re-layouts: 4.09 us -> 16.3 us
    all_to_all x1, waiting for transfers between devices: 77.5 us -> 67.7 us  [per_device(): lax.all_to_all(jnp.stack(jnp.split(acts, lax.axis_size('row'), axis=1)),...]
  transfers between devices with their start and end apart: 2 -> 2, of which waited for: 2 -> 2; matrix products, arithmetic and copies ran while one was open for 4% -> 8% of each run, Pallas kernels for 0% -> 0%
where the time goes in v1:
time: 268 us; the launch traced here: 267 us
  waiting for transfers between devices  119 us (44%)
  blocking collectives  82.2 us (31%)
  local copies, waits for them, and re-layouts  17 us (6%)
  other arithmetic  16.8 us (6%)
  between operations  15.4 us (6%)
  matrix products  9.58 us (4%)
  starting transfers between devices  7.21 us (3%)
    all_to_all x1, waiting for transfers between devices, per_device(): lax.all_to_all(jnp.stack(jnp.split(acts, lax.axis_size('row'), axis=1)),...  67.7 us
    all_gather x1, waiting for transfers between devices, per_device(): lax.all_gather(out_grads, 'row', axis=0, tiled=True)  50.4 us
    psum x1, blocking collectives, per_device(): update_total = lax.psum(jnp.sum(unclipped * unclipped), ('row', 'col'))  49.2 us
    psum x1, blocking collectives, per_device(): col_total = lax.psum(col_squares, 'row')  30.5 us
    unnamed x25, local copies, waits for them, and re-layouts  16.3 us
    dot_general x1, matrix products, per_device(): lax.dot_general(columns, lax.all_gather(out_grads, 'row', axis=0, tiled=T...  9.58 us
    sub x1, other arithmetic, per_device(): new_weight = weight - step_size * update  8.93 us
    all_to_all x1, starting transfers between devices, per_device(): lax.all_to_all(jnp.stack(jnp.split(acts, lax.axis_size('row'), axis=1)),...  7.17 us
  transfers between devices with their start and end apart: 2, of which 2 were waited for; matrix products, arithmetic and copies ran while one was open for 8% of the time, Pallas kernels for 0%

profile of v1, /device:TPU:12, one launch (start us, length us, event | category | flops | bytes accessed | tf_op | source)
XLA Modules:
  0.0 267.1 jit_solution(200129442536920540)
XLA Ops:
  7.2 0.7 all-gather.2.cloned.1.call-update
  7.9 1.6 bitcast_dynamic-update-slice_fusion.15
  9.5 1.6 bitcast_dynamic-update-slice_fusion.14
  11.0 1.6 bitcast_dynamic-update-slice_fusion.13
  12.6 1.6 bitcast_dynamic-update-slice_fusion.12
  14.2 1.6 bitcast_dynamic-update-slice_fusion.11
  15.8 1.6 bitcast_dynamic-update-slice_fusion.10
  17.3 1.6 bitcast_dynamic-update-slice_fusion.9
  18.9 0.7 bitcast_dynamic-update-slice_fusion.8
  19.6 0.7 bitcast_dynamic-update-slice_fusion.7
  20.2 0.7 bitcast_dynamic-update-slice_fusion.6
  20.9 0.7 bitcast_dynamic-update-slice_fusion.5
  21.5 0.7 bitcast_dynamic-update-slice_fusion.4
  22.2 0.7 bitcast_dynamic-update-slice_fusion.3
  24.9 7.2 %all-to-all-start = ((bf16[16,128,512]{2,1,0:T(8,128)(2,1)}), bf16[16,128,512]{2,1,0:T(8,128)(2,1)S(1)}, u32[]{:S(2)}, u32[]{:S(2)}) async-start(bf16[16,128,512]{2,1,0:T(8,128)(2,1)} %bitcast_dynamic-update-slice_fusion), calls=%async_computation | async-start | bytes 4194304 | tf_op jit(solution)/shard_map/all_to_all | solution.py:17
  32.0 3.9 %multiply_reduce_fusion.1 = f32[]{:T(128)} fusion(f32[512,2048]{1,0:T(8,128)} %param.7), kind=kLoop, calls=%fused_computation.4 | loop fusion | flops 2097151 | bytes 4194308 | tf_op jit(solution)/shard_map/reduce_sum | solution.py:29
  35.9 67.7 %all-to-all-done = bf16[16,128,512]{2,1,0:T(8,128)(2,1)S(1)} async-done(((bf16[16,128,512]{2,1,0:T(8,128)(2,1)}), bf16[16,128,512]{2,1,0:T(8,128)(2,1)S(1)}, u32[]{:S(2)}, u32[]{:S(2)}) %all-to-all-start) | async-done | bytes 2097184 | tf_op jit(solution)/shard_map/all_to_all | solution.py:17
  103.6 50.4 %all-gather.2.cloned.1.call-done = bf16[2048,2048]{1,0:T(8,128)(2,1)} async-done(((bf16[128,2048]{1,0:T(8,128)(2,1)}), bf16[2048,2048]{1,0:T(8,128)(2,1)}) %all-gather.2.cloned.1.call-update) | async-done | bytes 8388624 | tf_op jit(solution)/shard_map/all_gather | solution.py:22
  154.1 9.6 %fusion.1 = (f32[512]{0:T(512)S(1)}, f32[2048]{0:T(1024)S(1)}, f32[512,2048]{1,0:T(8,128)}) fusion(bf16[2048,512]{1,0:T(8,128)(2,1)S(1)} %bitcast.35, bf16[2048,2048]{1,0:T(8,128)(2,1)} %all-gather.2.cloned.1.call-done), kind=kOutput, calls=%fused_computation.6 | convolution fusion | flops 4299159040 | bytes 14690304 | tf_op jit(solution)/shard_map/dot_general | solution.py:20
  163.6 30.5 %psum.30 = f32[2048]{0:T(1024)S(1)} all-reduce(f32[2048]{0:T(1024)S(1)} %get-tuple-element.5), channel_id=1, replica_groups=mesh['row'=16,'col'=2] {'row'}, use_global_device_ids=true, to_apply=%region_5.0 | all-reduce | flops 2048 | bytes 16384 | tf_op jit(solution)/shard_map/psum | solution.py:31
  194.1 2.5 psum.29
  196.7 4.1 %multiply_reduce_fusion = f32[]{:T(128)} fusion(f32[512,2048]{1,0:T(8,128)} %get-tuple-element.10, f32[2048]{0:T(1024)S(1)} %multiply_add_fusion.1, f32[512]{0:T(512)S(1)} %multiply_add_fusion.2), kind=kLoop, calls=%fused_computation.1 | loop fusion | flops 4194303 | bytes 4204548 | tf_op jit(solution)/shard_map/reduce_sum | solution.py:36
  200.7 49.2 %all-reduce = (f32[]{:T(128)}, f32[]{:T(128)}) all-reduce(f32[]{:T(128)} %multiply_reduce_fusion, f32[]{:T(128)} %multiply_reduce_fusion.1), channel_id=1, replica_groups=mesh['row'=16,'col'=2] {'row','col'}, use_global_device_ids=true, to_apply=%region_7.0 | all-reduce | flops 2 | bytes 16 | tf_op jit(solution)/shard_map/psum | solution.py:36
  251.3 8.9 %multiply_subtract_fusion = (f32[512,2048]{1,0:T(8,128)}, f32[512,2048]{1,0:T(8,128)}) fusion(f32[512,2048]{1,0:T(8,128)} %param.7, f32[]{:T(128)S(6)} %mul_shard_map.3, f32[]{:T(128)S(6)} %max_shard_map.3, f32[512,2048]{1,0:T(8,128)} %get-tuple-element.10, f32[2048]{0:T(1024)S(1)} %multiply_add_fusion.1, f32[512]{0:T(512)S(1)} %multiply_add_fusion.2), kind=kLoop, calls=%fused_computation | loop fusion | flops 5242880 | bytes 16787464 | tf_op jit(solution)/shard_map/sub | solution.py:41
  (16 shorter events, 2.1 us)
Async XLA Ops:
  7.2 11.7 %copy-start = (bf16[128,8192]{1,0:T(8,128)(2,1)S(1)}, bf16[128,8192]{1,0:T(8,128)(2,1)}, u32[]{:S(2)}) copy-start(bf16[128,8192]{1,0:T(8,128)(2,1)} %param.5) | copy-start | bytes 6291460
  7.2 146.9 %all-gather.2.cloned.1.call-start = ((), (), s32[]{:S(2)}) async-start(), calls=%async_computation.1 | async-start | bytes 8912896 | tf_op jit(solution)/shard_map/all_gather | solution.py:22
  24.9 78.7 %all-to-all-start = ((bf16[16,128,512]{2,1,0:T(8,128)(2,1)}), bf16[16,128,512]{2,1,0:T(8,128)(2,1)S(1)}, u32[]{:S(2)}, u32[]{:S(2)}) async-start(bf16[16,128,512]{2,1,0:T(8,128)(2,1)} %bitcast_dynamic-update-slice_fusion), calls=%async_computation | async-start | bytes 4194304 | tf_op jit(solution)/shard_map/all_to_all | solution.py:17
  154.1 42.6 %copy-start.3 = (f32[2048]{0:T(1024)S(1)}, f32[2048]{0:T(1024)}, u32[]{:S(2)}) copy-start(f32[2048]{0:T(1024)} %param.9) | copy-start | bytes 24580
  154.1 42.6 %copy-start.4 = (f32[512]{0:T(512)S(1)}, f32[512]{0:T(512)}, u32[]{:S(2)}) copy-start(f32[512]{0:T(512)} %param.8) | copy-start | bytes 6148
  196.6 54.7 %copy-start.1 = (f32[2048]{0:T(1024)}, f32[2048]{0:T(1024)S(1)}, u32[]{:S(2)}) copy-start(f32[2048]{0:T(1024)S(1)} %multiply_add_fusion.1) | copy-start | bytes 24580
  196.7 54.6 %copy-start.2 = (f32[512]{0:T(512)}, f32[512]{0:T(512)S(1)}, u32[]{:S(2)}) copy-start(f32[512]{0:T(512)S(1)} %multiply_add_fusion.2) | copy-start | bytes 6148
Sparse Core Ops, SparseCore 0:
  10.8 143.2 all-gather.1
